TPU v7x, 32 devices: a whole 2x2x4 slice. The times are simulated.
32 devices in a mesh: mem: 4 (over x, core), lat: 8 (over z, y).
Axes of the slice: x: 2, y: 2, z: 4, core: 2. Of those that a mesh axis runs over, the one named last changes fastest.
Arguments:
- ensemble: float32 [256, 16, 512], P('mem', 'lat'), may hold values from -6 to 6
- diffusivity: float32 [16, 512], P('lat'), may hold values from 0.02 to 0.2
- north_wind: float32 [16, 512], P('lat'), may hold values from -0.25 to 0.25
- observed_blocks: int32 [8, 4, 4], P('lat'), may hold values from 0 to 7
- eastern_average_flags: int32 [8, 4, 512], P('lat'), may hold values 0 or 1
- observed_values: float32 [8, 4, 512], P('lat', 'mem'), may hold values from -6 to 6
- observed_error: float32 [8, 4, 512], P('lat', 'mem'), may hold values from 0.5 to 4
Outputs:
- analysis: float32 [256, 16, 512], P('mem', 'lat')
Inputs may be any that keep to these rules, and one draw needn't show every extreme that they name: `observed_blocks`: block i covers a band's flattened cells i * 128 to (i + 1) * 128 - 1; blocks may repeat.
All inputs are finite; a program needn't handle non-finite values. No bound on the sum of `eastern_average_flags` on one device may be relied on, other than what follows from the above.
Results may differ from a plain program's by a relative error of at most 0.0003.
Values sent between devices are 32-bit elements; how exact they have to be, the bound alone decides.
No kernel may reach another device: no remote copies, remote signals or barrier semaphores. Data moves between devices by JAX's collectives and lax.ppermute only.
A program may use at most 64 MiB of HBM per device.

v0:
```python
import jax
import jax.numpy as jnp
from jax import lax
from jax.sharding import PartitionSpec as P

OBS = 512
BLOCK = 128
NEWTON = 4
ADVECTION = 0.1
HIGHEST = lax.Precision.HIGHEST


def with_halo(block, sides, width):
    for axis, dim in sides:
        count = lax.axis_size(axis)
        forward = [(i, i + 1) for i in range(count - 1)]
        backward = [(target, source) for source, target in forward]
        low = lax.ppermute(
            lax.slice_in_dim(block, block.shape[dim] - width, None, axis=dim), axis, forward
        )
        high = lax.ppermute(lax.slice_in_dim(block, 0, width, axis=dim), axis, backward)
        block = jnp.concatenate([low, block, high], axis=dim)
    return block


def advance(padded, diffusivity, north_wind):
    centre = padded[:, 1:-1, :]
    northern = padded[:, :-2, :]
    equatorward_side = padded[:, 2:, :]
    eastern = jnp.roll(centre, -1, axis=2)
    western_neighbour = jnp.roll(centre, 1, axis=2)
    return (
        centre
        - ADVECTION * centre * (eastern - western_neighbour)
        - north_wind * (equatorward_side - northern)
        + diffusivity * (eastern + western_neighbour + northern + equatorward_side - 4.0 * centre)
    )


def contract_first(left, right):
    return lax.dot_general(
        left, right, (((0,), (0,)), ((), ())), precision=HIGHEST, preferred_element_type=jnp.float32
    )


def patch_gain(cell_values, seen_values, values, errors):
    sample_states = cell_values.shape[0]
    cell_offset = cell_values - jnp.mean(cell_values, axis=0)
    seen_mean = jnp.mean(seen_values, axis=0)
    seen_offset = seen_values - seen_mean
    covariance = contract_first(seen_offset, seen_offset) / (sample_states - 1.0) + jnp.diag(errors)
    row_scale = jnp.sum(jnp.abs(covariance), axis=1)
    inverse = jnp.diag(1.0 / row_scale)
    for sweep in range(NEWTON):
        product = jnp.dot(
            covariance, inverse, precision=HIGHEST, preferred_element_type=jnp.float32
        )
        inverse = 2.0 * inverse - jnp.dot(
            inverse, product, precision=HIGHEST, preferred_element_type=jnp.float32
        )
    cross_cov = contract_first(cell_offset, seen_offset) / (sample_states - 1.0)
    gain = jnp.dot(cross_cov, inverse, precision=HIGHEST, preferred_element_type=jnp.float32)
    innovation = values - seen_mean
    return (gain, innovation, seen_mean)


def body(
    ensemble,
    diffusivity,
    north_wind,
    observed_blocks,
    eastern_average_flags,
    observed_values,
    observed_error,
):
    local_members, row_count, meridian_total = ensemble.shape
    patch_count = lax.axis_size("mem")
    cell_count = row_count * meridian_total // patch_count
    coefficients = jnp.stack([diffusivity, north_wind])
    coef_rims = with_halo(coefficients, (("lat", 1),), 1)
    widened = with_halo(ensemble, (("lat", 1),), 2)
    variable_layers = advance(advance(widened, coef_rims[0], coef_rims[1]), diffusivity, north_wind)
    block_tiles = variable_layers.reshape(local_members, row_count * meridian_total // BLOCK, BLOCK)
    east_tiles = jnp.roll(variable_layers, -1, axis=2).reshape(
        local_members, row_count * meridian_total // BLOCK, BLOCK
    )
    chosen = observed_blocks[0].reshape(-1)
    direct = jnp.take(block_tiles, chosen, axis=1).reshape(local_members, patch_count, OBS)
    shifted = jnp.take(east_tiles, chosen, axis=1).reshape(local_members, patch_count, OBS)
    observed = jnp.where(eastern_average_flags[0][None] == 1, 0.5 * (direct + shifted), direct)
    owned = variable_layers.reshape(local_members, patch_count, cell_count)
    cell_values, seen_values = (
        lax.all_to_all(owned, "mem", split_axis=1, concat_axis=0, tiled=True),
        lax.all_to_all(observed, "mem", split_axis=1, concat_axis=0, tiled=True),
    )
    cell_values = cell_values[:, 0, :]
    seen_values = seen_values[:, 0, :]
    gain, innovation, seen_mean = patch_gain(
        cell_values, seen_values, observed_values[0, 0], observed_error[0, 0]
    )
    weights = innovation[None, :] - 0.5 * (seen_values - seen_mean[None, :])
    update = lax.dot_general(
        weights,
        gain,
        (((1,), (1,)), ((), ())),
        precision=HIGHEST,
        preferred_element_type=jnp.float32,
    )
    analysed = (cell_values + update)[:, None, :]
    returned = lax.all_to_all(analysed, "mem", split_axis=0, concat_axis=1, tiled=True)
    return returned.reshape(local_members, row_count, meridian_total)


def solution(mesh):
    return jax.shard_map(
        body,
        mesh=mesh,
        in_specs=(
            P("mem", "lat", None),
            P("lat", None),
            P("lat", None),
            P("lat", None, None),
            P("lat", None, None),
            P("lat", "mem", None),
            P("lat", "mem", None),
        ),
        out_specs=P("mem", "lat", None),
        check_vma=False,
    )
```

profile of v0, /device:TPU:0, one launch (start us, length us, event | category | flops | bytes accessed | tf_op | source)
XLA Modules:
  0.0 85.1 jit_solution(7209250416968997480)
XLA Ops:
  0.0 4.9 %collective-permute-start = (f32[64,2,512]{2,1,0:T(2,128)}, f32[64,2,512]{2,1,0:T(2,128)S(1)}, u32[]{:S(2)}, u32[]{:S(2)}) collective-permute-start(f32[64,2,512]{2,1,0:T(2,128)} %param.9), channel_id=1, source_target_pairs={{0,1},{1,2},{2,3},{3,4},{4,5},{5,6},{6,7},{8,9},{9,10},{10,11},{11... | collective-permute-start | bytes 786440 | tf_op jit(solution)/shard_map/ppermute | solution.py:18
  4.9 1.3 %collective-permute-start.1 = (f32[64,2,512]{2,1,0:T(2,128)}, f32[64,2,512]{2,1,0:T(2,128)S(1)}, u32[]{:S(2)}, u32[]{:S(2)}) collective-permute-start(f32[64,2,512]{2,1,0:T(2,128)} %param.9), channel_id=1, source_target_pairs={{1,0},{2,1},{3,2},{4,3},{5,4},{6,5},{7,6},{9,8},{10,9},{11,10},{12... | collective-permute-start | bytes 786440 | tf_op jit(solution)/shard_map/ppermute | solution.py:21
  7.0 4.5 %collective-permute-start.2 = (f32[2,1,512]{2,1,0:T(1,128)S(1)}, f32[2,1,512]{2,1,0:T(1,128)S(1)}, u32[]{:S(2)}, u32[]{:S(2)}) collective-permute-start(f32[2,1,512]{2,1,0:T(1,128)S(1)} %get-tuple-element.14), channel_id=1, source_target_pairs={{0,1},{1,2},{2,3},{3,4},{4,5},{5,6},{6,7},{8,9},{9,10},{10,11},{11... | collective-permute-start | bytes 12296 | tf_op jit(solution)/shard_map/ppermute | solution.py:18
  11.6 1.3 %collective-permute-start.3 = (f32[2,1,512]{2,1,0:T(1,128)S(1)}, f32[2,1,512]{2,1,0:T(1,128)S(1)}, u32[]{:S(2)}, u32[]{:S(2)}) collective-permute-start(f32[2,1,512]{2,1,0:T(1,128)S(1)} %get-tuple-element.15), channel_id=1, source_target_pairs={{1,0},{2,1},{3,2},{4,3},{5,4},{6,5},{7,6},{9,8},{10,9},{11,10},{12... | collective-permute-start | bytes 12296 | tf_op jit(solution)/shard_map/ppermute | solution.py:21
  13.0 3.5 %collective-permute-done.2 = f32[2,1,512]{2,1,0:T(1,128)S(1)} collective-permute-done((f32[2,1,512]{2,1,0:T(1,128)S(1)}, f32[2,1,512]{2,1,0:T(1,128)S(1)}, u32[]{:S(2)}, u32[]{:S(2)}) %collective-permute-start.2) | collective-permute-done | bytes 4128 | tf_op jit(solution)/shard_map/ppermute | solution.py:18
  16.5 1.0 %collective-permute-done.3 = f32[2,1,512]{2,1,0:T(1,128)S(1)} collective-permute-done((f32[2,1,512]{2,1,0:T(1,128)S(1)}, f32[2,1,512]{2,1,0:T(1,128)S(1)}, u32[]{:S(2)}, u32[]{:S(2)}) %collective-permute-start.3) | collective-permute-done | bytes 4128 | tf_op jit(solution)/shard_map/ppermute | solution.py:21
  17.5 1.3 %pad_maximum_fusion = f32[64,6,512]{2,1,0:T(8,128)S(1)} fusion(f32[64,2,512]{2,1,0:T(2,128)S(1)} %collective-permute-done.1, f32[64,2,512]{2,1,0:T(2,128)} %param.9, f32[64,2,512]{2,1,0:T(2,128)S(1)} %collective-permute-done), kind=kLoop, calls=%fused_computation.18 | loop fusion | flops 393216 | bytes 1572864 | tf_op jit(solution)/shard_map/concatenate | solution.py:22
  19.8 1.3 %multiply_add_fusion = f32[64,4,512]{2,1,0:T(4,128)S(1)} fusion(f32[64,2,512]{2,1,0:T(2,128)S(1)} %copy-done, f32[64,2,512]{2,1,0:T(2,128)S(1)} %collective-permute-done, f32[64,2,512]{2,1,0:T(2,128)S(1)} %collective-permute-done.1, f32[64,4,511]{2,1,0:T(4,128)S(1)} %get-tuple-element.7, f32[64,4,511]{2,1,0:T(4,128)S(1)} %get-tuple-element.6, ...), kind=kLoop, calls=%fused_computation.42 | loop fusion | flops 2883584 | bytes 2897920 | tf_op jit(solution)/shard_map/add | solution.py:33
  27.0 3.4 %all-to-all-start = ((f32[64,4,256]{2,0,1:T(8,128)}), f32[64,4,256]{2,0,1:T(8,128)S(1)}, u32[]{:S(2)}, u32[]{:S(2)}) async-start(f32[64,4,256]{2,0,1:T(8,128)} %copy.36), calls=%async_computation | async-start | bytes 524288 | tf_op jit(solution)/shard_map/all_to_all | solution.py:93
  30.6 1.0 %copy.41 = f32[64,4,512]{2,0,1:T(8,128)} copy(f32[64,4,512]{2,1,0:T(4,128)S(1)} %multiply_select_fusion) | data formatting | bytes 1048576 | tf_op jit(solution)/shard_map/jit(_where)/select_n | solution.py:90
  31.6 4.8 %all-to-all-done = f32[64,4,256]{2,0,1:T(8,128)S(1)} async-done(((f32[64,4,256]{2,0,1:T(8,128)}), f32[64,4,256]{2,0,1:T(8,128)S(1)}, u32[]{:S(2)}, u32[]{:S(2)}) %all-to-all-start) | async-done | bytes 262176 | tf_op jit(solution)/shard_map/all_to_all | solution.py:93
  36.4 3.6 %all-to-all-start.1 = ((f32[64,4,512]{2,0,1:T(8,128)}), f32[64,4,512]{2,0,1:T(8,128)S(1)}, u32[]{:S(2)}, u32[]{:S(2)}) async-start(f32[64,4,512]{2,0,1:T(8,128)} %copy.41), calls=%async_computation.1 | async-start | bytes 1048576 | tf_op jit(solution)/shard_map/all_to_all | solution.py:94
  40.1 8.5 %all-to-all-done.1 = f32[64,4,512]{2,0,1:T(8,128)S(1)} async-done(((f32[64,4,512]{2,0,1:T(8,128)}), f32[64,4,512]{2,0,1:T(8,128)S(1)}, u32[]{:S(2)}, u32[]{:S(2)}) %all-to-all-start.1) | async-done | bytes 524320 | tf_op jit(solution)/shard_map/all_to_all | solution.py:94
  50.0 1.2 %abs_reduce_fusion = (f32[512]{0:T(512)S(1)}, f32[512,512]{0,1:T(8,128)S(1)}) fusion(f32[512]{0:T(512)S(1)} %bitcast.94, f32[64,4,512]{2,0,1:T(8,128)S(1)} %all-to-all-done.1, f32[512]{0:T(512)S(1)} %get-tuple-element.17), kind=kOutput, calls=%fused_computation.19 | convolution fusion | flops 807009792 | bytes 1579008 | tf_op jit(solution)/shard_map/dot_general | solution.py:41
  51.2 3.5 %fusion.2 = f32[512,512]{1,0:T(8,128)S(1)} fusion(f32[512,512]{0,1:T(8,128)S(1)} %get-tuple-element.21, f32[512]{0:T(512)S(1)} %broadcast_divide_fusion), kind=kOutput, calls=%fused_computation.4 | convolution fusion | flops 1611137024 | bytes 2099200 | tf_op jit(solution)/shard_map/dot_general | solution.py:55
  54.7 1.9 %fusion.4 = f32[512,512]{0,1:T(8,128)S(1)} fusion(f32[512,512]{1,0:T(8,128)S(1)} %fusion.2, f32[512]{0:T(512)S(1)} %broadcast_divide_fusion), kind=kOutput, calls=%fused_computation.7 | convolution fusion | flops 1612185600 | bytes 2099200 | tf_op jit(solution)/shard_map/dot_general | solution.py:58
  56.6 3.5 %fusion.32 = f32[512,512]{1,0:T(8,128)S(1)} fusion(f32[512,512]{0,1:T(8,128)S(1)} %get-tuple-element.21, f32[512,512]{0,1:T(8,128)S(1)} %fusion.4), kind=kOutput, calls=%fused_computation.72 | convolution fusion | flops 1610612736 | bytes 3145728 | tf_op jit(solution)/shard_map/dot_general | solution.py:55
  60.1 1.9 %convolution_subtract_fusion.2 = f32[512,512]{0,1:T(8,128)S(1)} fusion(f32[512,512]{0,1:T(8,128)S(1)} %fusion.4, f32[512,512]{1,0:T(8,128)S(1)} %fusion.32), kind=kOutput, calls=%fused_computation.10 | convolution fusion | flops 1611137024 | bytes 3145728 | tf_op jit(solution)/shard_map/dot_general | solution.py:58
  62.0 3.7 %fusion.33 = f32[512,512]{1,0:T(8,128)S(1)} fusion(f32[512,512]{0,1:T(8,128)S(1)} %get-tuple-element.21, f32[512,512]{0,1:T(8,128)S(1)} %convolution_subtract_fusion.2), kind=kOutput, calls=%fused_computation.73 | convolution fusion | flops 1610612736 | bytes 3145728 | tf_op jit(solution)/shard_map/dot_general | solution.py:55
  65.7 1.9 %convolution_subtract_fusion.1 = f32[512,512]{0,1:T(8,128)S(1)} fusion(f32[512,512]{0,1:T(8,128)S(1)} %convolution_subtract_fusion.2, f32[512,512]{1,0:T(8,128)S(1)} %fusion.33), kind=kOutput, calls=%fused_computation.9 | convolution fusion | flops 1611137024 | bytes 3145728 | tf_op jit(solution)/shard_map/dot_general | solution.py:58
  67.5 3.5 %fusion.34 = f32[512,512]{1,0:T(8,128)S(1)} fusion(f32[512,512]{0,1:T(8,128)S(1)} %get-tuple-element.21, f32[512,512]{0,1:T(8,128)S(1)} %convolution_subtract_fusion.1), kind=kOutput, calls=%fused_computation.74 | convolution fusion | flops 1610612736 | bytes 3145728 | tf_op jit(solution)/shard_map/dot_general | solution.py:55
  71.0 1.9 %convolution_subtract_fusion = f32[512,512]{0,1:T(8,128)S(1)} fusion(f32[512,512]{0,1:T(8,128)S(1)} %convolution_subtract_fusion.1, f32[512,512]{1,0:T(8,128)S(1)} %fusion.34), kind=kOutput, calls=%fused_computation.8 | convolution fusion | flops 1611137024 | bytes 3145728 | tf_op jit(solution)/shard_map/dot_general | solution.py:58
  73.6 1.1 %fusion.35 = f32[256,512]{1,0:T(8,128)S(1)} fusion(f32[256,512]{1,0:T(8,128)S(1)} %fusion.9, f32[512,512]{0,1:T(8,128)S(1)} %convolution_subtract_fusion), kind=kOutput, calls=%fused_computation.75 | convolution fusion | flops 805306368 | bytes 2097152 | tf_op jit(solution)/shard_map/dot_general | solution.py:62
  75.6 8.4 %all_to_all.45 = f32[256,1,256]{2,1,0:T(1,128)S(1)} all-to-all(f32[256,1,256]{2,1,0:T(1,128)S(1)} %copy.46), channel_id=1, replica_groups=mesh['mem'=4,'lat'=8] {'mem'}, dimensions={0} | all-to-all | bytes 524288 | tf_op jit(solution)/shard_map/all_to_all | solution.py:110
  (56 shorter events, 12.0 us)
Async XLA Ops:
  0.0 17.5 %collective-permute-start = (f32[64,2,512]{2,1,0:T(2,128)}, f32[64,2,512]{2,1,0:T(2,128)S(1)}, u32[]{:S(2)}, u32[]{:S(2)}) collective-permute-start(f32[64,2,512]{2,1,0:T(2,128)} %param.9), channel_id=1, source_target_pairs={{0,1},{1,2},{2,3},{3,4},{4,5},{5,6},{6,7},{8,9},{9,10},{10,11},{11... | collective-permute-start | bytes 786440 | tf_op jit(solution)/shard_map/ppermute | solution.py:18
  4.9 12.6 %collective-permute-start.1 = (f32[64,2,512]{2,1,0:T(2,128)}, f32[64,2,512]{2,1,0:T(2,128)S(1)}, u32[]{:S(2)}, u32[]{:S(2)}) collective-permute-start(f32[64,2,512]{2,1,0:T(2,128)} %param.9), channel_id=1, source_target_pairs={{1,0},{2,1},{3,2},{4,3},{5,4},{6,5},{7,6},{9,8},{10,9},{11,10},{12... | collective-permute-start | bytes 786440 | tf_op jit(solution)/shard_map/ppermute | solution.py:21
  6.2 6.7 %copy-start.4 = (s32[1,4,4]{2,1,0:T(4,128)S(1)}, s32[1,4,4]{2,1,0:T(4,128)}, u32[]{:S(2)}) copy-start(s32[1,4,4]{2,1,0:T(4,128)} %param.12) | copy-start | bytes 196
  7.0 6.0 %copy-start.3 = (s32[1,4,512]{2,1,0:T(4,128)S(1)}, s32[1,4,512]{2,1,0:T(4,128)}, u32[]{:S(2)}) copy-start(s32[1,4,512]{2,1,0:T(4,128)} %param.13) | copy-start | bytes 24580
  7.0 9.5 %collective-permute-start.2 = (f32[2,1,512]{2,1,0:T(1,128)S(1)}, f32[2,1,512]{2,1,0:T(1,128)S(1)}, u32[]{:S(2)}, u32[]{:S(2)}) collective-permute-start(f32[2,1,512]{2,1,0:T(1,128)S(1)} %get-tuple-element.14), channel_id=1, source_target_pairs={{0,1},{1,2},{2,3},{3,4},{4,5},{5,6},{6,7},{8,9},{9,10},{10,11},{11... | collective-permute-start | bytes 12296 | tf_op jit(solution)/shard_map/ppermute | solution.py:18
  11.6 5.9 %collective-permute-start.3 = (f32[2,1,512]{2,1,0:T(1,128)S(1)}, f32[2,1,512]{2,1,0:T(1,128)S(1)}, u32[]{:S(2)}, u32[]{:S(2)}) collective-permute-start(f32[2,1,512]{2,1,0:T(1,128)S(1)} %get-tuple-element.15), channel_id=1, source_target_pairs={{1,0},{2,1},{3,2},{4,3},{5,4},{6,5},{7,6},{9,8},{10,9},{11,10},{12... | collective-permute-start | bytes 12296 | tf_op jit(solution)/shard_map/ppermute | solution.py:21
  13.0 4.5 %copy-start.2 = (f32[2,512]{1,0:T(2,128)S(1)}, f32[2,512]{1,0:T(2,128)}, u32[]{:S(2)}) copy-start(f32[2,512]{1,0:T(2,128)} %param.11) | copy-start | bytes 12292
  13.0 4.5 %copy-start.1 = (f32[2,512]{1,0:T(2,128)S(1)}, f32[2,512]{1,0:T(2,128)}, u32[]{:S(2)}) copy-start(f32[2,512]{1,0:T(2,128)} %param.10) | copy-start | bytes 12292
  18.8 1.0 %copy-start = (f32[64,2,512]{2,1,0:T(2,128)S(1)}, f32[64,2,512]{2,1,0:T(2,128)}, u32[]{:S(2)}) copy-start(f32[64,2,512]{2,1,0:T(2,128)} %param.9) | copy-start | bytes 786436
  27.0 9.4 %all-to-all-start = ((f32[64,4,256]{2,0,1:T(8,128)}), f32[64,4,256]{2,0,1:T(8,128)S(1)}, u32[]{:S(2)}, u32[]{:S(2)}) async-start(f32[64,4,256]{2,0,1:T(8,128)} %copy.36), calls=%async_computation | async-start | bytes 524288 | tf_op jit(solution)/shard_map/all_to_all | solution.py:93
  36.4 12.3 %all-to-all-start.1 = ((f32[64,4,512]{2,0,1:T(8,128)}), f32[64,4,512]{2,0,1:T(8,128)S(1)}, u32[]{:S(2)}, u32[]{:S(2)}) async-start(f32[64,4,512]{2,0,1:T(8,128)} %copy.41), calls=%async_computation.1 | async-start | bytes 1048576 | tf_op jit(solution)/shard_map/all_to_all | solution.py:94
  48.7 0.7 copy-start.5
  49.3 0.7 copy-start.6
where the time goes:
time: 85.7 us; the launch traced here: 85.1 us
  matrix products  25.2 us (29%)
  starting transfers between devices  19.1 us (22%)
  waiting for transfers between devices  17.8 us (21%)
  local copies, waits for them, and re-layouts  9.31 us (11%)
  blocking collectives  8.39 us (10%)
  other arithmetic  4.96 us (6%)
    dot_general x4, matrix products, patch_gain(): jnp.dot(covariance, inverse, precision=HIGHEST, preferred_element_type=jn...  14.1 us
    ppermute x2, starting transfers between devices, with_halo(): lax.ppermute(lax.slice_in_dim(block, block.shape[dim] - width, None, axis...  9.45 us
    all_to_all x1, waiting for transfers between devices, body(): lax.all_to_all(observed, 'mem', split_axis=1, concat_axis=0, tiled=True)  8.54 us
    all_to_all x1, blocking collectives, body(): lax.all_to_all(analysed, 'mem', split_axis=0, concat_axis=1, tiled=True)  8.39 us
    dot_general x4, matrix products, patch_gain(): jnp.dot(inverse, product, precision=HIGHEST, preferred_element_type=jnp.f...  7.55 us
    all_to_all x1, waiting for transfers between devices, body(): lax.all_to_all(owned, 'mem', split_axis=1, concat_axis=0, tiled=True)  4.83 us
    all_to_all x1, starting transfers between devices, body(): lax.all_to_all(observed, 'mem', split_axis=1, concat_axis=0, tiled=True)  3.65 us
    ppermute x2, waiting for transfers between devices, with_halo(): lax.ppermute(lax.slice_in_dim(block, block.shape[dim] - width, None, axis...  3.46 us
  transfers between devices with their start and end apart: 6, of which 4 were waited for; matrix products, arithmetic and copies ran while one was open for 2% of the time, Pallas kernels for 0%

commit v1 on v0

--- a/solution.py
+++ b/solution.py
@@ -8,6 +8,29 @@
 NEWTON = 4
 ADVECTION = 0.1
 HIGHEST = lax.Precision.HIGHEST
+
+
+def split_up(x, dim, size):
+    before, after = (x.shape[:dim], x.shape[dim + 1 :])
+    return jnp.moveaxis(x.reshape(*before, size, -1, *after), dim, 0)
+
+
+def joined_along(blocks, dim):
+    blocks = jnp.moveaxis(blocks, 0, dim)
+    shape = blocks.shape
+    return blocks.reshape(*shape[:dim], shape[dim] * shape[dim + 1], *shape[dim + 2 :])
+
+
+def exchange_directly(x, axis, split_dim, concat_dim):
+    size, position = (lax.axis_size(axis), lax.axis_index(axis))
+    blocks = split_up(x, split_dim, size)
+    out = blocks
+    for step in range(1, size):
+        target, source = ((position + step) % size, (position - step) % size)
+        sent = lax.dynamic_index_in_dim(blocks, target, 0)
+        other = lax.ppermute(sent, axis, [(i, (i + step) % size) for i in range(size)])
+        out = lax.dynamic_update_slice_in_dim(out, other, source, axis=0)
+    return joined_along(out, concat_dim)
 
 
 def with_halo(block, sides, width):
@@ -91,7 +114,7 @@
     owned = variable_layers.reshape(local_members, patch_count, cell_count)
     cell_values, seen_values = (
         lax.all_to_all(owned, "mem", split_axis=1, concat_axis=0, tiled=True),
-        lax.all_to_all(observed, "mem", split_axis=1, concat_axis=0, tiled=True),
+        exchange_directly(observed, "mem", 1, 0),
     )
     cell_values = cell_values[:, 0, :]
     seen_values = seen_values[:, 0, :]

time: 85.7 us -> 76.6 us (0.89)
  waiting for transfers between devices: 17.8 us -> 4 us
  local copies, waits for them, and re-layouts: 9.31 us -> 12.6 us
    all_to_all x1 -> x0, waiting for transfers between devices: 8.54 us -> none  [body(): lax.all_to_all(observed, 'mem', split_axis=1, concat_axis=0, tiled=True)]
    all_to_all x1, waiting for transfers between devices: 4.83 us -> 0.01 us  [body(): lax.all_to_all(owned, 'mem', split_axis=1, concat_axis=0, tiled=True)]
    dynamic_update_slice x0 -> x4, local copies, waits for them, and re-layouts: none -> 4.11 us  [exchange_directly(): out = lax.dynamic_update_slice_in_dim(out, other, source, axis=0)]
    all_to_all x1 -> x0, starting transfers between devices: 3.65 us -> none  [body(): lax.all_to_all(observed, 'mem', split_axis=1, concat_axis=0, tiled=True)]
    ppermute x0 -> x3, starting transfers between devices: none -> 3 us  [exchange_directly(): lax.ppermute(sent, axis, [(i, (i + step) % size) for i in range(size)])]
    select_n x1 -> x0, local copies, waits for them, and re-layouts: 0.95 us -> none  [body(): jnp.where(eastern_average_flags[0][None] == 1, 0.5 * (direct + shifted),...]
    ppermute x2, starting transfers between devices: 9.45 us -> 10.4 us  [with_halo(): lax.ppermute(lax.slice_in_dim(block, block.shape[dim] - width, None, axis...]
  transfers between devices with their start and end apart: 6 -> 8, of which waited for: 4 -> 2; matrix products, arithmetic and copies ran while one was open for 2% -> 39% of each run, Pallas kernels for 0% -> 0%
where the time goes in v1:
time: 76.6 us; the launch traced here: 76.1 us
  matrix products  25.5 us (33%)
  starting transfers between devices  19.3 us (25%)
  local copies, waits for them, and re-layouts  12.6 us (16%)
  blocking collectives  9.04 us (12%)
  other arithmetic  5.11 us (7%)
  waiting for transfers between devices  4 us (5%)
    dot_general x4, matrix products, patch_gain(): jnp.dot(covariance, inverse, precision=HIGHEST, preferred_element_type=jn...  13.9 us
    ppermute x2, starting transfers between devices, with_halo(): lax.ppermute(lax.slice_in_dim(block, block.shape[dim] - width, None, axis...  10.4 us
    all_to_all x1, blocking collectives, body(): lax.all_to_all(analysed, 'mem', split_axis=0, concat_axis=1, tiled=True)  9.04 us
    dot_general x4, matrix products, patch_gain(): jnp.dot(inverse, product, precision=HIGHEST, preferred_element_type=jnp.f...  7.79 us
    dynamic_update_slice x4, local copies, waits for them, and re-layouts, exchange_directly(): out = lax.dynamic_update_slice_in_dim(out, other, source, axis=0)  4.11 us
    all_to_all x1, starting transfers between devices, body(): lax.all_to_all(owned, 'mem', split_axis=1, concat_axis=0, tiled=True)  3.41 us
    ppermute x2, waiting for transfers between devices, with_halo(): lax.ppermute(lax.slice_in_dim(block, block.shape[dim] - width, None, axis...  3.4 us
    ppermute x3, starting transfers between devices, exchange_directly(): lax.ppermute(sent, axis, [(i, (i + step) % size) for i in range(size)])  3 us
  transfers between devices with their start and end apart: 8, of which 2 were waited for; matrix products, arithmetic and copies ran while one was open for 39% of the time, Pallas kernels for 0%

profile of v1, /device:TPU:0, one launch (start us, length us, event | category | flops | bytes accessed | tf_op | source)
XLA Modules:
  0.0 76.1 jit_solution(10931681252120149754)
XLA Ops:
  0.0 1.3 %collective-permute-start.1 = (f32[64,2,512]{2,1,0:T(2,128)}, f32[64,2,512]{2,1,0:T(2,128)S(1)}, u32[]{:S(2)}, u32[]{:S(2)}) collective-permute-start(f32[64,2,512]{2,1,0:T(2,128)} %param.9), channel_id=1, source_target_pairs={{1,0},{2,1},{3,2},{4,3},{5,4},{6,5},{7,6},{9,8},{10,9},{11,10},{12... | collective-permute-start | bytes 786440 | tf_op jit(solution)/shard_map/ppermute | solution.py:44
  1.3 5.5 %collective-permute-start = (f32[64,2,512]{2,1,0:T(2,128)}, f32[64,2,512]{2,1,0:T(2,128)S(1)}, u32[]{:S(2)}, u32[]{:S(2)}) collective-permute-start(f32[64,2,512]{2,1,0:T(2,128)} %param.9), channel_id=1, source_target_pairs={{0,1},{1,2},{2,3},{3,4},{4,5},{5,6},{6,7},{8,9},{9,10},{10,11},{11... | collective-permute-start | bytes 786440 | tf_op jit(solution)/shard_map/ppermute | solution.py:41
  7.6 4.8 %collective-permute-start.2 = (f32[2,1,512]{2,1,0:T(1,128)S(1)}, f32[2,1,512]{2,1,0:T(1,128)S(1)}, u32[]{:S(2)}, u32[]{:S(2)}) collective-permute-start(f32[2,1,512]{2,1,0:T(1,128)S(1)} %get-tuple-element.17), channel_id=1, source_target_pairs={{0,1},{1,2},{2,3},{3,4},{4,5},{5,6},{6,7},{8,9},{9,10},{10,11},{11... | collective-permute-start | bytes 12296 | tf_op jit(solution)/shard_map/ppermute | solution.py:41
  12.5 1.3 %collective-permute-start.3 = (f32[2,1,512]{2,1,0:T(1,128)S(1)}, f32[2,1,512]{2,1,0:T(1,128)S(1)}, u32[]{:S(2)}, u32[]{:S(2)}) collective-permute-start(f32[2,1,512]{2,1,0:T(1,128)S(1)} %get-tuple-element.18), channel_id=1, source_target_pairs={{1,0},{2,1},{3,2},{4,3},{5,4},{6,5},{7,6},{9,8},{10,9},{11,10},{12... | collective-permute-start | bytes 12296 | tf_op jit(solution)/shard_map/ppermute | solution.py:44
  14.0 3.4 %collective-permute-done.2 = f32[2,1,512]{2,1,0:T(1,128)S(1)} collective-permute-done((f32[2,1,512]{2,1,0:T(1,128)S(1)}, f32[2,1,512]{2,1,0:T(1,128)S(1)}, u32[]{:S(2)}, u32[]{:S(2)}) %collective-permute-start.2) | collective-permute-done | bytes 4128 | tf_op jit(solution)/shard_map/ppermute | solution.py:41
  18.0 1.3 %pad_maximum_fusion = f32[64,6,512]{2,1,0:T(8,128)S(1)} fusion(f32[64,2,512]{2,1,0:T(2,128)S(1)} %collective-permute-done.1, f32[64,2,512]{2,1,0:T(2,128)} %param.9, f32[64,2,512]{2,1,0:T(2,128)S(1)} %collective-permute-done), kind=kLoop, calls=%fused_computation.18 | loop fusion | flops 393216 | bytes 1572864 | tf_op jit(solution)/shard_map/concatenate | solution.py:45
  20.3 1.3 %multiply_add_fusion = f32[64,4,512]{2,1,0:T(4,128)S(1)} fusion(f32[64,2,512]{2,1,0:T(2,128)S(1)} %copy-done, f32[64,2,512]{2,1,0:T(2,128)S(1)} %collective-permute-done, f32[64,2,512]{2,1,0:T(2,128)S(1)} %collective-permute-done.1, f32[64,4,511]{2,1,0:T(4,128)S(1)} %get-tuple-element.7, f32[64,4,511]{2,1,0:T(4,128)S(1)} %get-tuple-element.6, ...), kind=kLoop, calls=%fused_computation.40 | loop fusion | flops 2883584 | bytes 2897920 | tf_op jit(solution)/shard_map/add | solution.py:56
  27.1 1.6 %collective-permute-start.5 = (f32[1,64,1,512]{3,0,1,2:T(1,128)S(1)}, f32[1,64,1,512]{3,0,1,2:T(1,128)S(1)}, u32[]{:S(2)}, u32[]{:S(2)}) collective-permute-start(f32[1,64,1,512]{3,0,1,2:T(1,128)S(1)} %get-tuple-element.9), channel_id=1, source_target_pairs={{0,16},{8,24},{16,0},{24,8},{1,17},{9,25},{17,1},{25,9},{2,18},{10... | collective-permute-start | bytes 393224 | tf_op jit(solution)/shard_map/ppermute | solution.py:31
  28.6 1.4 %collective-permute-start.6 = (f32[1,64,1,512]{3,0,1,2:T(1,128)S(1)}, f32[1,64,1,512]{3,0,1,2:T(1,128)S(1)}, u32[]{:S(2)}, u32[]{:S(2)}) collective-permute-start(f32[1,64,1,512]{3,0,1,2:T(1,128)S(1)} %get-tuple-element.8), channel_id=1, source_target_pairs={{0,24},{8,0},{16,8},{24,16},{1,25},{9,1},{17,9},{25,17},{2,26},{10... | collective-permute-start | bytes 393224 | tf_op jit(solution)/shard_map/ppermute | solution.py:31
  31.0 3.4 %all-to-all-start = ((f32[64,4,256]{2,0,1:T(8,128)}), f32[64,4,256]{2,0,1:T(8,128)S(1)}, u32[]{:S(2)}, u32[]{:S(2)}) async-start(f32[64,4,256]{2,0,1:T(8,128)} %copy.36), calls=%async_computation | async-start | bytes 524288 | tf_op jit(solution)/shard_map/all_to_all | solution.py:116
  34.5 1.3 %dynamic_update_slice.9 = f32[4,64,1,512]{3,0,1,2:T(4,128)S(1)} dynamic-update-slice(f32[4,64,1,512]{3,0,1,2:T(4,128)S(1)} %bitcast.76, f32[1,64,1,512]{3,0,1,2:T(1,128)S(1)} %collective-permute-done.4, s32[]{:T(128)S(6)} %select_n.76, s32[]{:T(128)} %constant.84.clone.1, s32[]{:T(128)} %constant.84.clone.1, s32[]{:T(128)} %constant.84.clone.1) | dynamic-update-slice | bytes 262148 | tf_op jit(solution)/shard_map/dynamic_update_slice | solution.py:32
  35.7 1.3 %dynamic_update_slice.10 = f32[4,64,1,512]{3,0,1,2:T(4,128)S(1)} dynamic-update-slice(f32[4,64,1,512]{3,0,1,2:T(4,128)S(1)} %dynamic_update_slice.9, f32[1,64,1,512]{3,0,1,2:T(1,128)S(1)} %collective-permute-done.5, s32[]{:T(128)S(6)} %select_n.80, s32[]{:T(128)} %constant.84.clone.1, s32[]{:T(128)} %constant.84.clone.1, s32[]{:T(128)} %constant.84.clone.1) | dynamic-update-slice | bytes 262148 | tf_op jit(solution)/shard_map/dynamic_update_slice | solution.py:32
  37.0 1.4 %dynamic_update_slice.11 = f32[4,64,1,512]{3,0,1,2:T(4,128)S(1)} dynamic-update-slice(f32[4,64,1,512]{3,0,1,2:T(4,128)S(1)} %dynamic_update_slice.10, f32[1,64,1,512]{3,0,1,2:T(1,128)S(1)} %collective-permute-done.6, s32[]{:T(128)S(6)} %select_n.84, s32[]{:T(128)} %constant.84.clone.1, s32[]{:T(128)} %constant.84.clone.1, s32[]{:T(128)} %constant.84.clone.1) | dynamic-update-slice | bytes 262148 | tf_op jit(solution)/shard_map/dynamic_update_slice | solution.py:32
  40.0 1.3 %abs_reduce_fusion = (f32[512]{0:T(512)S(1)}, f32[512,512]{0,1:T(8,128)S(1)}) fusion(f32[512]{0:T(512)S(1)} %bitcast.84, f32[4,64,512]{2,0,1:T(4,128)S(1)} %subtract_bitcast_fusion), kind=kOutput, calls=%fused_computation.19 | convolution fusion | flops 806878720 | bytes 1576960 | tf_op jit(solution)/shard_map/dot_general | solution.py:64
  41.4 3.5 %fusion.2 = f32[512,512]{1,0:T(8,128)S(1)} fusion(f32[512,512]{0,1:T(8,128)S(1)} %get-tuple-element.24, f32[512]{0:T(512)S(1)} %broadcast_divide_fusion), kind=kOutput, calls=%fused_computation.4 | convolution fusion | flops 1611137024 | bytes 2099200 | tf_op jit(solution)/shard_map/dot_general | solution.py:78
  44.8 1.9 %fusion.4 = f32[512,512]{0,1:T(8,128)S(1)} fusion(f32[512,512]{1,0:T(8,128)S(1)} %fusion.2, f32[512]{0:T(512)S(1)} %broadcast_divide_fusion), kind=kOutput, calls=%fused_computation.7 | convolution fusion | flops 1612185600 | bytes 2099200 | tf_op jit(solution)/shard_map/dot_general | solution.py:81
  46.7 3.5 %fusion.30 = f32[512,512]{1,0:T(8,128)S(1)} fusion(f32[512,512]{0,1:T(8,128)S(1)} %get-tuple-element.24, f32[512,512]{0,1:T(8,128)S(1)} %fusion.4), kind=kOutput, calls=%fused_computation.73 | convolution fusion | flops 1610612736 | bytes 3145728 | tf_op jit(solution)/shard_map/dot_general | solution.py:78
  50.2 2.1 %convolution_subtract_fusion.2 = f32[512,512]{0,1:T(8,128)S(1)} fusion(f32[512,512]{0,1:T(8,128)S(1)} %fusion.4, f32[512,512]{1,0:T(8,128)S(1)} %fusion.30), kind=kOutput, calls=%fused_computation.10 | convolution fusion | flops 1611137024 | bytes 3145728 | tf_op jit(solution)/shard_map/dot_general | solution.py:81
  52.4 3.5 %fusion.31 = f32[512,512]{1,0:T(8,128)S(1)} fusion(f32[512,512]{0,1:T(8,128)S(1)} %get-tuple-element.24, f32[512,512]{0,1:T(8,128)S(1)} %convolution_subtract_fusion.2), kind=kOutput, calls=%fused_computation.74 | convolution fusion | flops 1610612736 | bytes 3145728 | tf_op jit(solution)/shard_map/dot_general | solution.py:78
  55.8 1.9 %convolution_subtract_fusion.1 = f32[512,512]{0,1:T(8,128)S(1)} fusion(f32[512,512]{0,1:T(8,128)S(1)} %convolution_subtract_fusion.2, f32[512,512]{1,0:T(8,128)S(1)} %fusion.31), kind=kOutput, calls=%fused_computation.9 | convolution fusion | flops 1611137024 | bytes 3145728 | tf_op jit(solution)/shard_map/dot_general | solution.py:81
  57.7 3.5 %fusion.32 = f32[512,512]{1,0:T(8,128)S(1)} fusion(f32[512,512]{0,1:T(8,128)S(1)} %get-tuple-element.24, f32[512,512]{0,1:T(8,128)S(1)} %convolution_subtract_fusion.1), kind=kOutput, calls=%fused_computation.75 | convolution fusion | flops 1610612736 | bytes 3145728 | tf_op jit(solution)/shard_map/dot_general | solution.py:78
  61.2 1.9 %convolution_subtract_fusion = f32[512,512]{0,1:T(8,128)S(1)} fusion(f32[512,512]{0,1:T(8,128)S(1)} %convolution_subtract_fusion.1, f32[512,512]{1,0:T(8,128)S(1)} %fusion.32), kind=kOutput, calls=%fused_computation.8 | convolution fusion | flops 1611137024 | bytes 3145728 | tf_op jit(solution)/shard_map/dot_general | solution.py:81
  64.0 1.1 %fusion.33 = f32[256,512]{1,0:T(8,128)S(1)} fusion(f32[256,512]{1,0:T(8,128)S(1)} %fusion.9, f32[512,512]{0,1:T(8,128)S(1)} %convolution_subtract_fusion), kind=kOutput, calls=%fused_computation.76 | convolution fusion | flops 805306368 | bytes 2097152 | tf_op jit(solution)/shard_map/dot_general | solution.py:85
  66.0 9.0 %all_to_all.30 = f32[256,1,256]{2,1,0:T(1,128)S(1)} all-to-all(f32[256,1,256]{2,1,0:T(1,128)S(1)} %copy.49), channel_id=1, replica_groups=mesh['mem'=4,'lat'=8] {'mem'}, dimensions={0} | all-to-all | bytes 524288 | tf_op jit(solution)/shard_map/all_to_all | solution.py:133
  (65 shorter events, 13.2 us)
Async XLA Ops:
  0.0 18.0 %collective-permute-start.1 = (f32[64,2,512]{2,1,0:T(2,128)}, f32[64,2,512]{2,1,0:T(2,128)S(1)}, u32[]{:S(2)}, u32[]{:S(2)}) collective-permute-start(f32[64,2,512]{2,1,0:T(2,128)} %param.9), channel_id=1, source_target_pairs={{1,0},{2,1},{3,2},{4,3},{5,4},{6,5},{7,6},{9,8},{10,9},{11,10},{12... | collective-permute-start | bytes 786440 | tf_op jit(solution)/shard_map/ppermute | solution.py:44
  1.3 16.7 %collective-permute-start = (f32[64,2,512]{2,1,0:T(2,128)}, f32[64,2,512]{2,1,0:T(2,128)S(1)}, u32[]{:S(2)}, u32[]{:S(2)}) collective-permute-start(f32[64,2,512]{2,1,0:T(2,128)} %param.9), channel_id=1, source_target_pairs={{0,1},{1,2},{2,3},{3,4},{4,5},{5,6},{6,7},{8,9},{9,10},{10,11},{11... | collective-permute-start | bytes 786440 | tf_op jit(solution)/shard_map/ppermute | solution.py:41
  6.8 6.9 %copy-start.4 = (s32[1,4,4]{2,1,0:T(4,128)S(1)}, s32[1,4,4]{2,1,0:T(4,128)}, u32[]{:S(2)}) copy-start(s32[1,4,4]{2,1,0:T(4,128)} %param.12) | copy-start | bytes 196
  7.6 6.2 %copy-start.3 = (s32[1,4,512]{2,1,0:T(4,128)S(1)}, s32[1,4,512]{2,1,0:T(4,128)}, u32[]{:S(2)}) copy-start(s32[1,4,512]{2,1,0:T(4,128)} %param.13) | copy-start | bytes 24580
  7.6 9.7 %collective-permute-start.2 = (f32[2,1,512]{2,1,0:T(1,128)S(1)}, f32[2,1,512]{2,1,0:T(1,128)S(1)}, u32[]{:S(2)}, u32[]{:S(2)}) collective-permute-start(f32[2,1,512]{2,1,0:T(1,128)S(1)} %get-tuple-element.17), channel_id=1, source_target_pairs={{0,1},{1,2},{2,3},{3,4},{4,5},{5,6},{6,7},{8,9},{9,10},{10,11},{11... | collective-permute-start | bytes 12296 | tf_op jit(solution)/shard_map/ppermute | solution.py:41
  12.5 5.5 %collective-permute-start.3 = (f32[2,1,512]{2,1,0:T(1,128)S(1)}, f32[2,1,512]{2,1,0:T(1,128)S(1)}, u32[]{:S(2)}, u32[]{:S(2)}) collective-permute-start(f32[2,1,512]{2,1,0:T(1,128)S(1)} %get-tuple-element.18), channel_id=1, source_target_pairs={{1,0},{2,1},{3,2},{4,3},{5,4},{6,5},{7,6},{9,8},{10,9},{11,10},{12... | collective-permute-start | bytes 12296 | tf_op jit(solution)/shard_map/ppermute | solution.py:44
  13.9 4.0 %copy-start.2 = (f32[2,512]{1,0:T(2,128)S(1)}, f32[2,512]{1,0:T(2,128)}, u32[]{:S(2)}) copy-start(f32[2,512]{1,0:T(2,128)} %param.11) | copy-start | bytes 12292
  14.0 4.0 %copy-start.1 = (f32[2,512]{1,0:T(2,128)S(1)}, f32[2,512]{1,0:T(2,128)}, u32[]{:S(2)}) copy-start(f32[2,512]{1,0:T(2,128)} %param.10) | copy-start | bytes 12292
  19.3 1.0 %copy-start = (f32[64,2,512]{2,1,0:T(2,128)S(1)}, f32[64,2,512]{2,1,0:T(2,128)}, u32[]{:S(2)}) copy-start(f32[64,2,512]{2,1,0:T(2,128)} %param.9) | copy-start | bytes 786436
  27.0 7.4 %collective-permute-start.4 = (f32[1,64,1,512]{3,0,1,2:T(1,128)S(1)}, f32[1,64,1,512]{3,0,1,2:T(1,128)S(1)}, u32[]{:S(2)}, u32[]{:S(2)}) collective-permute-start(f32[1,64,1,512]{3,0,1,2:T(1,128)S(1)} %get-tuple-element.10), channel_id=1, source_target_pairs={{0,8},{8,16},{16,24},{24,0},{1,9},{9,17},{17,25},{25,1},{2,10},{10... | collective-permute-start | bytes 393224 | tf_op jit(solution)/shard_map/ppermute | solution.py:31
  27.1 8.6 %collective-permute-start.5 = (f32[1,64,1,512]{3,0,1,2:T(1,128)S(1)}, f32[1,64,1,512]{3,0,1,2:T(1,128)S(1)}, u32[]{:S(2)}, u32[]{:S(2)}) collective-permute-start(f32[1,64,1,512]{3,0,1,2:T(1,128)S(1)} %get-tuple-element.9), channel_id=1, source_target_pairs={{0,16},{8,24},{16,0},{24,8},{1,17},{9,25},{17,1},{25,9},{2,18},{10... | collective-permute-start | bytes 393224 | tf_op jit(solution)/shard_map/ppermute | solution.py:31
  28.6 8.4 %collective-permute-start.6 = (f32[1,64,1,512]{3,0,1,2:T(1,128)S(1)}, f32[1,64,1,512]{3,0,1,2:T(1,128)S(1)}, u32[]{:S(2)}, u32[]{:S(2)}) collective-permute-start(f32[1,64,1,512]{3,0,1,2:T(1,128)S(1)} %get-tuple-element.8), channel_id=1, source_target_pairs={{0,24},{8,0},{16,8},{24,16},{1,25},{9,1},{17,9},{25,17},{2,26},{10... | collective-permute-start | bytes 393224 | tf_op jit(solution)/shard_map/ppermute | solution.py:31
  31.0 32.1 %all-to-all-start = ((f32[64,4,256]{2,0,1:T(8,128)}), f32[64,4,256]{2,0,1:T(8,128)S(1)}, u32[]{:S(2)}, u32[]{:S(2)}) async-start(f32[64,4,256]{2,0,1:T(8,128)} %copy.36), calls=%async_computation | async-start | bytes 524288 | tf_op jit(solution)/shard_map/all_to_all | solution.py:116
  38.6 0.7 copy-start.5
  39.3 0.7 copy-start.6
